TPU v7x, 256 devices: a whole 4x4x8 slice. The times are simulated.
256 devices in a mesh: req: 32 (over z, x), tp: 8 (over y, core).
Axes of the slice: x: 4, y: 4, z: 8, core: 2. Of those that a mesh axis runs over, the one named last changes fastest.
Arguments:
- hidden_in: bfloat16 [192, 64, 3072], P('req', None, 'tp'), may hold values from -3 to 3
- request_order: int32 [192], replicated, may hold values from 0 to 191, as said below
- norm_gain: bfloat16 [3072], replicated, may hold values from 0.099609375 to 1.8984375
- w_query: bfloat16 [3072, 3072], P(None, 'tp'), may hold values from -0.109375 to 0.109375
- key_weight: bfloat16 [3072, 1024], P(None, 'tp'), may hold values from -0.4375 to 0.4375
- value_weight: bfloat16 [3072, 1024], P(None, 'tp'), may hold values from -0.109375 to 0.109375
- w_out: bfloat16 [3072, 3072], P('tp'), may hold values from -0.109375 to 0.109375
- key_cache: bfloat16 [192, 8, 3456, 128], P('req', 'tp'), may hold values from -360 to 360
- cached_values: bfloat16 [192, 8, 3456, 128], P('req', 'tp'), may hold values from -24 to 24
- cache_lengths: int32 [192], P('req'), may hold values from 864 to 3456, as said below
- tree_parent: int32 [192, 64], P('req'), may hold values from 0 to 63, as said below
- kept_nodes: int32 [192, 8], P('req'), may hold values from 0 to 63
Outputs:
- layer_out: bfloat16 [192, 64, 3072], P('req', None, 'tp')
- appended: bfloat16 [192, 2, 8, 8, 128], P('req', None, None, 'tp')
Inputs may be any that keep to these rules, and one draw needn't show every extreme that they name: `request_order`: each request is held by exactly one slot. The 6 requests of one device's rows go to 6 different devices of req, and the slots of one device hold requests of 6 different devices. `cache_lengths`: some slot has exactly 3456 live positions. `tree_parent`: node 0 has parent 0; every other node's parent has a lower index.
All inputs are finite; a program needn't handle non-finite values.
Results may differ from a plain program's by a relative error of at most 0.0085.
The roundings to bfloat16 on the way count: a program that leaves them out, or rounds other values in their place, can miss the bound.
Values may be sent and summed in bfloat16 or wider, within the bound.
A program may use at most 128 MiB of HBM per device.

v0:
```python
import jax
import jax.numpy as jnp
from jax import lax
from jax.sharding import PartitionSpec as P

HEAD_WIDTH = 128
NORM_EPSILON = 1e-05


def rotary_embedding(vectors, token_positions):
    half_dim = vectors.shape[-1] // 2
    frequency = 500000.0 ** (-jnp.arange(half_dim, dtype=jnp.float32) * 2.0 / vectors.shape[-1])
    angles = token_positions[..., None] * frequency
    cosine = jnp.cos(angles)[..., None, :]
    sine = jnp.sin(angles)[..., None, :]
    first_half = vectors[..., :half_dim]
    second_half = vectors[..., half_dim:]
    return jnp.concatenate(
        [first_half * cosine - second_half * sine, second_half * cosine + first_half * sine],
        axis=-1,
    )


def body(
    hidden_in,
    request_order,
    norm_gain,
    w_query,
    key_weight,
    value_weight,
    w_out,
    key_cache,
    cached_values,
    cache_lengths,
    tree_parent,
    kept_nodes,
):
    slots_here = key_cache.shape[0]
    tree_length = hidden_in.shape[1]
    width_local = hidden_in.shape[2]
    local_groups = key_cache.shape[1]
    local_heads = w_query.shape[1] // HEAD_WIDTH
    group_width = local_heads // local_groups
    slot_ids = lax.axis_index("req") * slots_here + jnp.arange(slots_here, dtype=jnp.int32)
    own_order = request_order[slot_ids]
    piece = lax.all_gather(hidden_in, "req", axis=0, tiled=True)
    piece_ids = jnp.arange(piece.shape[0], dtype=jnp.int32)
    chooser = (own_order[:, None] == piece_ids[None, :]).astype(jnp.bfloat16)
    dealt = jnp.einsum("rm,mtd->rtd", chooser, piece, preferred_element_type=jnp.float32).astype(
        jnp.bfloat16
    )
    widened = lax.all_gather(dealt, "tp", axis=2, tiled=True).astype(jnp.float32)
    normalized_input = (
        widened
        * lax.rsqrt(jnp.mean(widened * widened, axis=-1, keepdims=True) + NORM_EPSILON)
        * norm_gain.astype(jnp.float32)
    ).astype(jnp.bfloat16)
    flat_rows = normalized_input.reshape(slots_here * tree_length, normalized_input.shape[2])
    query_rows = jnp.dot(flat_rows, w_query, preferred_element_type=jnp.float32).reshape(
        slots_here, tree_length, local_heads, HEAD_WIDTH
    )
    fresh_keys = jnp.dot(flat_rows, key_weight, preferred_element_type=jnp.float32).reshape(
        slots_here, tree_length, local_groups, HEAD_WIDTH
    )
    fresh_values = (
        jnp.dot(flat_rows, value_weight, preferred_element_type=jnp.float32)
        .astype(jnp.bfloat16)
        .reshape(slots_here, tree_length, local_groups, HEAD_WIDTH)
    )
    node_ids = jnp.arange(tree_length, dtype=jnp.int32)
    parent_link = (
        (tree_parent[:, :, None] == node_ids[None, None, :]) & (node_ids[None, :, None] > 0)
    ).astype(jnp.float32)
    ancestry = jnp.eye(tree_length, dtype=jnp.float32)[None] + parent_link
    for sweep in range(tree_length.bit_length()):
        ancestry = jnp.minimum(
            jnp.einsum("rij,rjk->rik", ancestry, ancestry, precision=lax.Precision.HIGHEST), 1.0
        )
    token_positions = cache_lengths.astype(jnp.float32)[:, None] + jnp.sum(ancestry, axis=-1) - 1.0
    rotated_query = (
        rotary_embedding(query_rows, token_positions)
        .astype(jnp.bfloat16)
        .reshape(slots_here, tree_length, local_groups, group_width, HEAD_WIDTH)
    )
    key_rot = rotary_embedding(fresh_keys, token_positions).astype(jnp.bfloat16)
    score_scale = HEAD_WIDTH ** (-0.5)
    cache_scores = (
        jnp.einsum(
            "rtgqd,rgcd->rgqtc", rotated_query, key_cache, preferred_element_type=jnp.float32
        )
        * score_scale
    )
    live_keys = jnp.arange(key_cache.shape[2], dtype=jnp.int32)[None, :] < cache_lengths[:, None]
    cache_scores = jnp.where(live_keys[:, None, None, None, :], cache_scores, -jnp.inf)
    tree_scores = (
        jnp.einsum("rtgqd,rsgd->rgqts", rotated_query, key_rot, preferred_element_type=jnp.float32)
        * score_scale
    )
    tree_scores = jnp.where(ancestry[:, None, None] > 0, tree_scores, -jnp.inf)
    row_max = jnp.maximum(jnp.max(cache_scores, axis=-1), jnp.max(tree_scores, axis=-1))
    cache_exp = jnp.exp(cache_scores - row_max[..., None])
    tree_exp = jnp.exp(tree_scores - row_max[..., None])
    row_total = jnp.sum(cache_exp, axis=-1) + jnp.sum(tree_exp, axis=-1)
    cache_weights = (cache_exp / row_total[..., None]).astype(jnp.bfloat16)
    tree_weights = (tree_exp / row_total[..., None]).astype(jnp.bfloat16)
    attended = jnp.einsum(
        "rgqtc,rgcd->rtgqd", cache_weights, cached_values, preferred_element_type=jnp.float32
    )
    attended = attended + jnp.einsum(
        "rgqts,rsgd->rtgqd", tree_weights, fresh_values, preferred_element_type=jnp.float32
    )
    attended = attended.astype(jnp.bfloat16).reshape(
        slots_here, tree_length, local_heads * HEAD_WIDTH
    )
    keep_select = (kept_nodes[:, :, None] == node_ids[None, None, :]).astype(jnp.bfloat16)
    stacked = jnp.stack([key_rot, fresh_values], axis=1)
    appended = jnp.einsum(
        "rkt,rxtgd->rxkgd", keep_select, stacked, preferred_element_type=jnp.float32
    ).astype(jnp.bfloat16)
    partials = jnp.dot(
        attended.reshape(-1, attended.shape[2]), w_out, preferred_element_type=jnp.float32
    )
    summed = lax.psum(partials, "tp")
    my_share = lax.dynamic_slice_in_dim(summed, lax.axis_index("tp") * width_local, width_local, 1)
    layer_out = (my_share.reshape(dealt.shape) + dealt.astype(jnp.float32)).astype(jnp.bfloat16)
    return (layer_out, appended)


def solution(mesh):
    placed = (
        P("req", None, "tp"),
        P(),
        P(),
        P(None, "tp"),
        P(None, "tp"),
        P(None, "tp"),
        P("tp", None),
        P("req", "tp", None, None),
        P("req", "tp", None, None),
        P("req"),
        P("req", None),
        P("req", None),
    )
    return jax.shard_map(
        body,
        mesh=mesh,
        in_specs=placed,
        out_specs=(P("req", None, "tp"), P("req", None, None, "tp", None)),
        check_vma=False,
    )
```

profile of v0, /device:TPU:2, one launch (start us, length us, event | category | flops | bytes accessed | tf_op | source)
XLA Modules:
  0.0 284.8 jit_solution(10960639715566622475)
XLA Ops:
  7.2 0.0 copy-start
  7.2 0.0 all-gather.3.cloned.1.call-start
  7.2 0.7 all-gather.3.cloned.1.call-update
  7.9 0.0 all-gather.5.cloned.1.call-start
  8.0 1.3 gather_fusion
  9.3 0.0 copy-start.4
  9.3 0.0 copy-start.3
  9.3 0.0 copy-start.5
  9.3 106.1 %all-gather.3.cloned.1.call-done = bf16[192,64,384]{2,1,0:T(8,128)(2,1)} async-done(((bf16[6,64,384]{2,1,0:T(8,128)(2,1)}), bf16[192,64,384]{2,1,0:T(8,128)(2,1)}) %all-gather.3.cloned.1.call-update) | async-done | bytes 9437200 | tf_op jit(solution)/shard_map/all_gather | solution.py:46
  115.4 11.9 %fusion.3 = bf16[6,64,384]{2,0,1:T(8,128)(2,1)S(1)} fusion(bf16[192,64,384]{2,1,0:T(8,128)(2,1)} %all-gather.3.cloned.1.call-done, s32[6]{0:T(128)S(1)} %gather_fusion), kind=kOutput, calls=%fused_computation.7 | convolution fusion | flops 56624256 | bytes 9732120 | tf_op jit(solution)/shard_map/rm,mtd->rtd/dot_general | solution.py:49
  127.3 0.8 copy.78
  128.1 0.0 all-gather.5.cloned.1.call-update
  128.1 0.0 all-reduce.2.cloned.1.call-start
  128.2 0.0 copy-done.4
  128.2 0.0 copy-done.3
  128.2 0.0 copy-done.5
  128.3 0.5 convolution_minimum_fusion.6
  128.7 0.3 convolution_minimum_fusion.5
  129.0 0.3 convolution_minimum_fusion.4
  129.4 0.3 convolution_minimum_fusion.3
  129.7 0.3 convolution_minimum_fusion.2
  130.0 0.3 convolution_minimum_fusion.1
  130.4 0.4 fusion.63
  130.8 0.1 copy.54
  131.0 4.5 %copy.51 = bf16[3072,384]{0,1:T(8,128)(2,1)} copy(bf16[3072,384]{1,0:T(8,128)(2,1)} %param.15) | data formatting | bytes 4718592 | tf_op args[3]
  135.5 0.1 add_add_fusion
  135.5 0.8 multiply_cosine_fusion.1
  136.3 0.1 iota_compare_fusion.1
  136.4 19.0 %all-gather.5.cloned.1.call-done = bf16[6,64,3072]{2,1,0:T(8,128)(2,1)} async-done(((bf16[6,64,384]{2,1,0:T(8,128)(2,1)}), bf16[6,64,3072]{2,1,0:T(8,128)(2,1)}) %all-gather.5.cloned.1.call-update) | async-done | bytes 2359312 | tf_op jit(solution)/shard_map/all_gather | solution.py:52
  155.4 0.0 copy-start.2
  155.4 0.0 copy-start.1
  155.4 2.4 fusion.11
  157.7 2.4 fusion.13
  160.2 0.0 copy-done.2
  160.2 0.0 slice-start
  160.2 0.8 convolution_bitcast_fusion
  161.0 0.8 fusion.38
  161.8 0.0 copy-done.1
  161.8 0.0 slice-start.1
  161.8 1.4 fusion.14
  163.2 0.3 subtract_convert_fusion
  163.6 0.0 slice-done
  163.6 0.0 slice-done.1
  163.6 6.9 %fusion.2 = (f32[6,3,64]{2,1,0:T(4,128)S(1)}, f32[6,64,3,3456]{3,1,2,0:T(8,128)}) fusion(pred[6,3456]{1,0:T(8,128)(4,1)S(1)} %iota_compare_fusion.1, bf16[6,1,3456,128]{3,2,1,0:T(8,128)(2,1)S(1)} %bitcast.146, bf16[6,64,3,64]{3,1,2,0:T(8,128)(2,1)S(1)} %get-tuple-element.11, bf16[6,64,3,64]{3,1,2,0:T(8,128)(2,1)S(1)} %get-tuple-element.10), kind=kOutput, calls=%fused_computation.6 | convolution fusion | flops 1031748480 | bytes 21553920 | tf_op jit(solution)/shard_map/rtgqd,rgcd->rgqtc/dot_general | solution.py:88
  170.5 0.4 fusion.64
  171.0 0.1 fusion.27
  171.1 9.2 %fusion.1 = f32[6,3,64]{2,1,0:T(4,128)S(1)} fusion(f32[6,64,3,3456]{3,1,2,0:T(8,128)} %get-tuple-element.19, f32[6,3,64]{2,1,0:T(4,128)S(1)} %max.9, pred[6,3456]{1,0:T(8,128)(4,1)S(1)} %iota_compare_fusion.1), kind=kLoop, calls=%fused_computation.5 | loop fusion | flops 15924096 | bytes 15955200 | tf_op jit(solution)/shard_map/reduce_sum | solution.py:103
  180.3 1.9 convolution_convert_fusion
  182.2 10.3 %fusion.17 = f32[6,128,3,64]{1,3,2,0:T(8,128)S(1)} fusion(bf16[6,1,3456,128]{3,2,1,0:T(8,128)(2,1)} %param.20, f32[6,3,64]{2,1,0:T(4,128)S(1)} %add.98, f32[6,3,64]{2,1,0:T(4,128)S(1)} %max.9, f32[6,64,3,3456]{3,1,2,0:T(8,128)} %get-tuple-element.19, pred[6,3456]{1,0:T(8,128)(4,1)S(1)} %iota_compare_fusion.1), kind=kOutput, calls=%fused_computation.25 | convolution fusion | flops 1039122432 | bytes 21853440 | tf_op jit(solution)/shard_map/rgqtc,rgcd->rtgqd/dot_general | solution.py:106
  192.5 0.3 fusion.24
  192.8 0.3 copy.56
  193.1 0.0 copy-done
  193.1 0.0 copy-start.6
  193.1 3.5 %fusion.28 = f32[384,3072]{1,0:T(8,128)} fusion(bf16[384,3072]{1,0:T(8,128)(2,1)S(1)} %copy-done, bf16[48,8,3,128]{3,2,1,0:T(4,128)(2,1)S(1)} %bitcast.149), kind=kOutput, calls=%fused_computation.48 | convolution fusion | flops 905969664 | bytes 7372800 | tf_op jit(solution)/shard_map/dot_general | solution.py:120
  196.7 0.0 all-reduce.2.cloned.1.call-update
  196.7 0.0 copy-done.6
  196.7 0.8 fusion.25
  197.5 78.8 %all-reduce.2.cloned.1.call-done = f32[384,3072]{1,0:T(8,128)} async-done(((f32[384,3072]{1,0:T(8,128)}), f32[384,3072]{1,0:T(8,128)}) %all-reduce.2.cloned.1.call-update) | async-done | bytes 4718608 | tf_op jit(solution)/shard_map/psum | solution.py:123
  276.3 1.1 constant_dynamic-slice_fusion
  277.4 0.8 add_convert_fusion
  (12 shorter events, 0.1 us)
Async XLA Ops:
  7.2 185.9 %copy-start = (bf16[384,3072]{1,0:T(8,128)(2,1)S(1)}, bf16[384,3072]{1,0:T(8,128)(2,1)}, u32[]{:S(2)}) copy-start(bf16[384,3072]{1,0:T(8,128)(2,1)} %param.18) | copy-start | bytes 7077892
  7.2 108.2 %all-gather.3.cloned.1.call-start = ((), (), s32[]{:S(2)}) async-start(), calls=%async_computation | async-start | bytes 9732096 | tf_op jit(solution)/shard_map/all_gather | solution.py:46
  7.9 147.5 %all-gather.5.cloned.1.call-start = ((), (), s32[]{:S(2)}) async-start(), calls=%async_computation.1 | async-start | bytes 2654208 | tf_op jit(solution)/shard_map/all_gather | solution.py:52
  9.3 118.9 %copy-start.4 = (s32[6]{0:T(128)S(1)}, s32[6]{0:T(128)}, u32[]{:S(2)}) copy-start(s32[6]{0:T(128)} %param.21) | copy-start | bytes 76
  9.3 118.9 %copy-start.3 = (bf16[3072]{0:T(1024)(128)(2,1)S(1)}, bf16[3072]{0:T(1024)(128)(2,1)}, u32[]{:S(2)}) copy-start(bf16[3072]{0:T(1024)(128)(2,1)} %param.14) | copy-start | bytes 18436
  9.3 118.9 %copy-start.5 = (s32[6,64]{1,0:T(8,128)S(1)}, s32[6,64]{1,0:T(8,128)}, u32[]{:S(2)}) copy-start(s32[6,64]{1,0:T(8,128)} %param.22) | copy-start | bytes 4612
  128.1 148.2 %all-reduce.2.cloned.1.call-start = ((), (), s32[]{:S(2)}) async-start(), calls=%async_computation.2 | async-start | bytes 9437184 | tf_op jit(solution)/shard_map/psum | solution.py:123
  155.4 4.8 %copy-start.2 = (bf16[3072,128]{1,0:T(8,128)(2,1)S(1)}, bf16[3072,128]{1,0:T(8,128)(2,1)}, u32[]{:S(2)}) copy-start(bf16[3072,128]{1,0:T(8,128)(2,1)} %param.16) | copy-start | bytes 2359300
  155.4 6.4 %copy-start.1 = (bf16[3072,384]{0,1:T(8,128)(2,1)S(1)}, bf16[3072,384]{0,1:T(8,128)(2,1)}, u32[]{:S(2)}) copy-start(bf16[3072,384]{0,1:T(8,128)(2,1)} %copy.51) | copy-start | bytes 7077892
  160.2 3.4 %slice-start = ((s8[5308416]{0:T(1024)(128)(4,1)}), s8[4194304]{0:T(1024)(128)(4,1)S(1)}, s32[]{:S(2)}) async-start(s8[5308416]{0:T(1024)(128)(4,1)} %bitcast.145), calls=%async_computation.3 | async-start | bytes 8388608
  161.8 1.7 slice-start.1
  193.1 3.6 %copy-start.6 = (s32[6,8]{1,0:T(8,128)S(1)}, s32[6,8]{1,0:T(8,128)}, u32[]{:S(2)}) copy-start(s32[6,8]{1,0:T(8,128)} %param.23) | copy-start | bytes 580
Sparse Core Ops, SparseCore 0:
  10.6 104.8 all-gather.2
  128.2 27.0 all-gather.4
  196.8 79.4 all-reduce.1
where the time goes:
time: 285 us
  waiting for transfers between devices  205 us (72%)
  matrix products  40.8 us (14%)
  other arithmetic  17 us (6%)
  between operations  14.1 us (5%)
  local copies, waits for them, and re-layouts  8.1 us (3%)
    all_gather x1, waiting for transfers between devices, body(): piece = lax.all_gather(hidden_in, 'req', axis=0, tiled=True)  106 us
    psum x1, waiting for transfers between devices, body(): summed = lax.psum(partials, 'tp')  78.8 us
    all_gather x1, waiting for transfers between devices, body(): lax.all_gather(dealt, 'tp', axis=2, tiled=True).astype(jnp.float32)  19 us
    dot_general x1, matrix products, body(): jnp.einsum('rm,mtd->rtd', chooser, piece, preferred_element_type=jnp.floa...  11.9 us
    dot_general x1, matrix products, body(): jnp.einsum('rgqtc,rgcd->rtgqd', cache_weights, cached_values, preferred_e...  10.3 us
    reduce_sum x2, other arithmetic, body(): row_total = jnp.sum(cache_exp, axis=-1) + jnp.sum(tree_exp, axis=-1)  9.32 us
    dot_general x1, matrix products, body(): jnp.einsum('rtgqd,rgcd->rgqtc', rotated_query, key_cache, preferred_eleme...  6.91 us
  transfers between devices with their start and end apart: 3, of which 3 were waited for; matrix products, arithmetic and copies ran while one was open for 4% of the time, Pallas kernels for 0%

commit v1 on v0

--- a/solution.py
+++ b/solution.py
@@ -120,7 +120,9 @@
     partials = jnp.dot(
         attended.reshape(-1, attended.shape[2]), w_out, preferred_element_type=jnp.float32
     )
-    summed = lax.psum(partials, "tp")
+    summed = partials
+    for hop in (1, 2, 4):
+        summed = summed + lax.ppermute(summed, "tp", [(dev, dev ^ hop) for dev in range(8)])
     my_share = lax.dynamic_slice_in_dim(summed, lax.axis_index("tp") * width_local, width_local, 1)
     layer_out = (my_share.reshape(dealt.shape) + dealt.astype(jnp.float32)).astype(jnp.bfloat16)
     return (layer_out, appended)

time: 285 us -> 425 us (1.49)
  waiting for transfers between devices: 205 us -> 340 us
  other arithmetic: 17 us -> 22.3 us
    ppermute x0 -> x3, waiting for transfers between devices: none -> 214 us  [body(): lax.ppermute(summed, 'tp', [(dev, dev ^ hop) for dev in range(8)])]
    psum x1 -> x0, waiting for transfers between devices: 78.8 us -> none  [body(): summed = lax.psum(partials, 'tp')]
    add x0 -> x3, other arithmetic: none -> 5.17 us  [body(): summed + lax.ppermute(summed, 'tp', [(dev, dev ^ hop) for dev in range(8)])]
  transfers between devices with their start and end apart: 3 -> 5, of which waited for: 3 -> 5; matrix products, arithmetic and copies ran while one was open for 4% -> 2% of each run, Pallas kernels for 0% -> 0%
where the time goes in v1:
time: 425 us; the launch traced here: 424 us
  waiting for transfers between devices  340 us (80%)
  matrix products  38.7 us (9%)
  other arithmetic  22.3 us (5%)
  between operations  14.4 us (3%)
  local copies, waits for them, and re-layouts  7.02 us (2%)
    ppermute x3, waiting for transfers between devices, body(): lax.ppermute(summed, 'tp', [(dev, dev ^ hop) for dev in range(8)])  214 us
    all_gather x1, waiting for transfers between devices, body(): piece = lax.all_gather(hidden_in, 'req', axis=0, tiled=True)  106 us
    all_gather x1, waiting for transfers between devices, body(): lax.all_gather(dealt, 'tp', axis=2, tiled=True).astype(jnp.float32)  19 us
    dot_general x1, matrix products, body(): jnp.einsum('rm,mtd->rtd', chooser, piece, preferred_element_type=jnp.floa...  11.9 us
    dot_general x1, matrix products, body(): jnp.einsum('rgqtc,rgcd->rtgqd', cache_weights, cached_values, preferred_e...  10.4 us
    reduce_sum x2, other arithmetic, body(): row_total = jnp.sum(cache_exp, axis=-1) + jnp.sum(tree_exp, axis=-1)  9.32 us
  transfers between devices with their start and end apart: 5, of which 5 were waited for; matrix products, arithmetic and copies ran while one was open for 2% of the time, Pallas kernels for 0%

profile of v1, /device:TPU:2, one launch (start us, length us, event | category | flops | bytes accessed | tf_op | source)
XLA Modules:
  0.0 424.3 jit_solution(4330064221997318670)
XLA Ops:
  7.2 0.0 copy-start
  7.2 0.0 all-gather.3.cloned.1.call-start
  7.2 0.7 all-gather.3.cloned.1.call-update
  7.9 0.0 all-gather.5.cloned.1.call-start
  8.0 1.3 gather_fusion
  9.3 0.0 copy-start.3
  9.3 0.0 copy-start.5
  9.3 106.1 %all-gather.3.cloned.1.call-done = bf16[192,64,384]{2,1,0:T(8,128)(2,1)} async-done(((bf16[6,64,384]{2,1,0:T(8,128)(2,1)}), bf16[192,64,384]{2,1,0:T(8,128)(2,1)}) %all-gather.3.cloned.1.call-update) | async-done | bytes 9437200 | tf_op jit(solution)/shard_map/all_gather | solution.py:46
  115.4 11.9 %fusion.3 = bf16[6,64,384]{2,0,1:T(8,128)(2,1)S(1)} fusion(bf16[192,64,384]{2,1,0:T(8,128)(2,1)} %all-gather.3.cloned.1.call-done, s32[6]{0:T(128)S(1)} %gather_fusion), kind=kOutput, calls=%fused_computation.7 | convolution fusion | flops 56624256 | bytes 9732120 | tf_op jit(solution)/shard_map/rm,mtd->rtd/dot_general | solution.py:49
  127.3 0.8 copy.78
  128.1 0.0 all-gather.5.cloned.1.call-update
  128.1 0.0 copy-done.4
  128.1 0.0 copy-done.3
  128.2 0.0 copy-done.5
  128.2 0.5 convolution_minimum_fusion.6
  128.7 0.3 convolution_minimum_fusion.5
  129.0 0.3 convolution_minimum_fusion.4
  129.3 0.3 convolution_minimum_fusion.3
  129.7 0.3 convolution_minimum_fusion.2
  130.0 0.3 convolution_minimum_fusion.1
  130.3 0.4 fusion.63
  130.8 0.1 copy.54
  130.9 4.5 %copy.51 = bf16[3072,384]{0,1:T(8,128)(2,1)} copy(bf16[3072,384]{1,0:T(8,128)(2,1)} %param.15) | data formatting | bytes 4718592 | tf_op args[3]
  135.4 0.1 add_add_fusion
  135.5 0.8 multiply_cosine_fusion.1
  136.3 0.1 iota_compare_fusion.1
  136.3 19.0 %all-gather.5.cloned.1.call-done = bf16[6,64,3072]{2,1,0:T(8,128)(2,1)} async-done(((bf16[6,64,384]{2,1,0:T(8,128)(2,1)}), bf16[6,64,3072]{2,1,0:T(8,128)(2,1)}) %all-gather.5.cloned.1.call-update) | async-done | bytes 2359312 | tf_op jit(solution)/shard_map/all_gather | solution.py:52
  155.3 0.0 copy-start.2
  155.3 2.3 fusion.11
  157.6 0.0 copy-start.1
  157.6 2.6 fusion.13
  160.2 0.0 copy-done.2
  160.2 0.0 slice-start
  160.2 0.8 convolution_bitcast_fusion
  161.0 0.8 fusion.38
  161.9 0.0 copy-done.1
  161.9 0.0 slice-start.1
  161.9 1.4 fusion.14
  163.3 0.3 subtract_convert_fusion
  163.6 0.0 slice-done
  163.6 0.0 slice-done.1
  163.6 6.9 %fusion.2 = (f32[6,3,64]{2,1,0:T(4,128)S(1)}, f32[6,64,3,3456]{3,1,2,0:T(8,128)}) fusion(pred[6,3456]{1,0:T(8,128)(4,1)S(1)} %iota_compare_fusion.1, bf16[6,1,3456,128]{3,2,1,0:T(8,128)(2,1)S(1)} %bitcast.146, bf16[6,64,3,64]{3,1,2,0:T(8,128)(2,1)S(1)} %get-tuple-element.11, bf16[6,64,3,64]{3,1,2,0:T(8,128)(2,1)S(1)} %get-tuple-element.10), kind=kOutput, calls=%fused_computation.6 | convolution fusion | flops 1031748480 | bytes 21553920 | tf_op jit(solution)/shard_map/rtgqd,rgcd->rgqtc/dot_general | solution.py:88
  170.5 0.4 fusion.64
  171.0 0.1 fusion.27
  171.1 9.2 %fusion.1 = f32[6,3,64]{2,1,0:T(4,128)S(1)} fusion(f32[6,64,3,3456]{3,1,2,0:T(8,128)} %get-tuple-element.19, f32[6,3,64]{2,1,0:T(4,128)S(1)} %max.9, pred[6,3456]{1,0:T(8,128)(4,1)S(1)} %iota_compare_fusion.1), kind=kLoop, calls=%fused_computation.5 | loop fusion | flops 15924096 | bytes 15955200 | tf_op jit(solution)/shard_map/reduce_sum | solution.py:103
  180.3 1.9 convolution_convert_fusion
  182.3 10.4 %fusion.17 = f32[6,128,3,64]{1,3,2,0:T(8,128)S(1)} fusion(bf16[6,1,3456,128]{3,2,1,0:T(8,128)(2,1)} %param.20, f32[6,3,64]{2,1,0:T(4,128)S(1)} %add.105, f32[6,3,64]{2,1,0:T(4,128)S(1)} %max.9, f32[6,64,3,3456]{3,1,2,0:T(8,128)} %get-tuple-element.19, pred[6,3456]{1,0:T(8,128)(4,1)S(1)} %iota_compare_fusion.1), kind=kOutput, calls=%fused_computation.25 | convolution fusion | flops 1039122432 | bytes 21853440 | tf_op jit(solution)/shard_map/rgqtc,rgcd->rtgqd/dot_general | solution.py:106
  192.6 0.3 fusion.24
  192.9 0.3 copy.56
  193.2 0.0 copy-done
  193.2 1.4 fusion.28
  194.6 0.3 collective-permute-start
  194.9 7.7 %collective-permute-done = f32[384,3072]{1,0:T(8,128)S(1)} collective-permute-done((f32[384,3072]{1,0:T(8,128)S(1)}, f32[384,3072]{1,0:T(8,128)S(1)}, u32[]{:S(2)}, u32[]{:S(2)}) %collective-permute-start) | collective-permute-done | bytes 4718624 | tf_op jit(solution)/shard_map/ppermute | solution.py:125
  202.6 1.0 add.107
  203.6 0.0 copy-start.6
  203.6 0.2 collective-permute-start.1
  203.8 103.8 %collective-permute-done.1 = f32[384,3072]{1,0:T(8,128)S(1)} collective-permute-done((f32[384,3072]{1,0:T(8,128)S(1)}, f32[384,3072]{1,0:T(8,128)S(1)}, u32[]{:S(2)}, u32[]{:S(2)}) %collective-permute-start.1) | collective-permute-done | bytes 4718624 | tf_op jit(solution)/shard_map/ppermute | solution.py:125
  307.6 2.9 add.108
  310.5 1.7 collective-permute-start.2
  312.2 0.0 copy-done.6
  312.2 0.8 fusion.25
  313.1 102.3 %collective-permute-done.2 = f32[384,3072]{1,0:T(8,128)} collective-permute-done((f32[384,3072]{1,0:T(8,128)}, f32[384,3072]{1,0:T(8,128)}, u32[]{:S(2)}, u32[]{:S(2)}) %collective-permute-start.2) | collective-permute-done | bytes 4718624 | tf_op jit(solution)/shard_map/ppermute | solution.py:125
  415.4 1.3 dynamic-slice_add_fusion
  416.7 0.8 add_convert_fusion
  (13 shorter events, 0.1 us)
Async XLA Ops:
  7.2 186.0 %copy-start = (bf16[384,3072]{1,0:T(8,128)(2,1)S(1)}, bf16[384,3072]{1,0:T(8,128)(2,1)}, u32[]{:S(2)}) copy-start(bf16[384,3072]{1,0:T(8,128)(2,1)} %param.18) | copy-start | bytes 7077892
  7.2 108.2 %all-gather.3.cloned.1.call-start = ((), (), s32[]{:S(2)}) async-start(), calls=%async_computation | async-start | bytes 9732096 | tf_op jit(solution)/shard_map/all_gather | solution.py:46
  7.9 147.4 %all-gather.5.cloned.1.call-start = ((), (), s32[]{:S(2)}) async-start(), calls=%async_computation.1 | async-start | bytes 2654208 | tf_op jit(solution)/shard_map/all_gather | solution.py:52
  9.3 118.8 %copy-start.4 = (s32[6]{0:T(128)S(1)}, s32[6]{0:T(128)}, u32[]{:S(2)}) copy-start(s32[6]{0:T(128)} %param.21) | copy-start | bytes 76
  9.3 118.8 %copy-start.3 = (bf16[3072]{0:T(1024)(128)(2,1)S(1)}, bf16[3072]{0:T(1024)(128)(2,1)}, u32[]{:S(2)}) copy-start(bf16[3072]{0:T(1024)(128)(2,1)} %param.14) | copy-start | bytes 18436
  9.3 118.9 %copy-start.5 = (s32[6,64]{1,0:T(8,128)S(1)}, s32[6,64]{1,0:T(8,128)}, u32[]{:S(2)}) copy-start(s32[6,64]{1,0:T(8,128)} %param.22) | copy-start | bytes 4612
  155.3 4.9 %copy-start.2 = (bf16[3072,128]{1,0:T(8,128)(2,1)S(1)}, bf16[3072,128]{1,0:T(8,128)(2,1)}, u32[]{:S(2)}) copy-start(bf16[3072,128]{1,0:T(8,128)(2,1)} %param.16) | copy-start | bytes 2359300
  157.6 4.2 copy-start.1
  160.2 3.4 slice-start
  161.9 1.7 slice-start.1
  194.6 8.0 %collective-permute-start = (f32[384,3072]{1,0:T(8,128)S(1)}, f32[384,3072]{1,0:T(8,128)S(1)}, u32[]{:S(2)}, u32[]{:S(2)}) collective-permute-start(f32[384,3072]{1,0:T(8,128)S(1)} %fusion.28), channel_id=1, source_target_pairs={{0,1},{1,0},{2,3},{3,2},{4,5},{5,4},{6,7},{7,6},{8,9},{9,8},{10,11... | collective-permute-start | bytes 14155784 | tf_op jit(solution)/shard_map/ppermute | solution.py:125
  203.6 108.6 %copy-start.6 = (s32[6,8]{1,0:T(8,128)S(1)}, s32[6,8]{1,0:T(8,128)}, u32[]{:S(2)}) copy-start(s32[6,8]{1,0:T(8,128)} %param.23) | copy-start | bytes 580
  203.6 104.0 %collective-permute-start.1 = (f32[384,3072]{1,0:T(8,128)S(1)}, f32[384,3072]{1,0:T(8,128)S(1)}, u32[]{:S(2)}, u32[]{:S(2)}) collective-permute-start(f32[384,3072]{1,0:T(8,128)S(1)} %add.107), channel_id=1, source_target_pairs={{0,2},{1,3},{2,0},{3,1},{4,6},{5,7},{6,4},{7,5},{8,10},{9,11},{10,... | collective-permute-start | bytes 14155784 | tf_op jit(solution)/shard_map/ppermute | solution.py:125
  310.5 104.9 %collective-permute-start.2 = (f32[384,3072]{1,0:T(8,128)}, f32[384,3072]{1,0:T(8,128)}, u32[]{:S(2)}, u32[]{:S(2)}) collective-permute-start(f32[384,3072]{1,0:T(8,128)} %add.108), channel_id=1, source_target_pairs={{0,4},{1,5},{2,6},{3,7},{4,0},{5,1},{6,2},{7,3},{8,12},{9,13},{10,... | collective-permute-start | bytes 14155784 | tf_op jit(solution)/shard_map/ppermute | solution.py:125
Sparse Core Ops, SparseCore 0:
  10.6 104.8 all-gather.2
  128.2 27.0 all-gather.4
